TPU v7x, 128 devices: a whole 4x4x4 slice. The times are simulated.
128 devices in a mesh: gx: 16 (over z, x), gy: 8 (over y, core).
Axes of the slice: x: 4, y: 4, z: 4, core: 2. Of those that a mesh axis runs over, the one named last changes fastest.
Arguments:
- cotangent: float32 [16, 8, 42, 1024], P('gx', 'gy'), may hold values from -6 to 6
- section_states: bfloat16 [3, 16, 8, 42, 1024], P(None, 'gx', 'gy'), may hold values from -6 to 6
- inverse_area: float32 [16, 8, 1024], P('gx', 'gy'), may hold values from 0.5 to 2
- edge_length: float32 [16, 8, 3, 1024], P('gx', 'gy'), may hold values from 0.5 to 1.5
- roughness: float32 [16, 8, 1024], P('gx', 'gy'), may hold values from 0.5 to 2
- soil_conductance: float32 [16, 8, 1024], P('gx', 'gy'), may hold values from 0.5 to 2
- zone_friction: float32 [512], replicated, may hold values from 0.25 to 1
- zone_conductivity: float32 [512], replicated, may hold values from 0.25 to 1
- wet_mask: int32 [16, 8, 1024], P('gx', 'gy'), may hold values 0 or 1
- element_zone: int32 [16, 8, 1024], P('gx', 'gy'), may hold values from 0 to 511, as said below
- send_face: int32 [16, 8, 8, 256], P('gx', 'gy'), may hold values from 0 to 3071, as said below
- send_count: int32 [16, 8, 8], P('gx', 'gy'), may hold values from 0 to 256, as said below
- face_partner: int32 [16, 8, 3, 1024], P('gx', 'gy'), may hold values from 0 to 4867, as said below
- volume_matrix: float32 [12, 12], replicated, may hold values from -1.75 to 1.75
- flux_in: float32 [8, 8], replicated, may hold values from -2 to 2
- flux_out: float32 [8, 8], replicated, may hold values from -2 to 2
Outputs:
- adjoint: float32 [16, 8, 42, 1024], P('gx', 'gy')
- zone_grads: float32 [2, 512], replicated
Inputs may be any that keep to these rules, and one draw needn't show every extreme that they name: `element_zone`: zones lie near their partition: an element of partition (a, b) has a zone among the 8 zones from (a*8+b)*4 on, modulo 512. send_count[a, b, n] equals send_count of the partition at offset n for offset 7 - n; it is 0 where that partition lies outside the grid, 1 to 4 for the four diagonal offsets (4 for some pair in every draw), at least 192 for the others, and 256 for some pair in every draw. `send_face`: the live slots of a partition name distinct faces; slots at or beyond the count hold 0. `face_partner`: the faces are paired: a face sent in slot j to offset n faces entry 3072 + n*256 + j, the other faces face a local face whose partner they are, or themselves.
All inputs are finite; a program needn't handle non-finite values. No bound on the sum of `wet_mask` on one device may be relied on, other than what follows from the above.
Results may differ from a plain program's by a relative error of at most 0.0003.
Values may be sent and summed in bfloat16 or wider, within the bound.
A program may use at most 64 MiB of HBM per device.

v0:
```python
import jax
import jax.numpy as jnp
import numpy as np
from jax import lax
from jax.sharding import PartitionSpec as P

LAYERS = 10
ZONE_DEV = 4
TIME_STEP = 0.2
SALT_RETURN = 0.5
LATERAL = 0.5
GRAD_WEIGHT = 1.0 / 64.0
FACE_NODES = ((1, 2), (2, 0), (0, 1))
MOMENTUM_ROWS = np.array([0, 0, 0, 1, 1, 1, 1, 1, 1, 0, 0, 0], np.float32)


def shifted(x, axis, by):
    peers = lax.axis_size(axis)
    pairs = [(i, i + by) for i in range(peers) if 0 <= i + by < peers]
    return lax.ppermute(x, axis, pairs)


def trace_rows():
    channels = 8 + 2 * LAYERS
    rows = np.zeros((channels, 3), np.int32)
    for face_no in range(3):
        for end_no in range(2):
            node_no = FACE_NODES[face_no][end_no]
            for comp_no in range(4):
                rows[comp_no * 2 + end_no, face_no] = comp_no * 3 + node_no
            for layer_no in range(LAYERS):
                rows[8 + layer_no * 2 + end_no, face_no] = 12 + layer_no * 3 + node_no
    return rows.reshape(-1)


def take_traces(state, rows):
    channels = rows.shape[0] // 3
    return state[rows].reshape(channels, 3 * state.shape[1])


def lift_back(flux, rows, row_count):
    return jnp.zeros((row_count, flux.shape[-1]), jnp.float32).at[rows].add(flux)


def section_speed(flat_traces, outer_flat):
    return jnp.sqrt(1.0 + 0.25 * jnp.mean(flat_traces[:8] ** 2 + outer_flat[:8] ** 2, axis=0))


def local_operator(
    state,
    received,
    conductivity,
    friction,
    wave_speed,
    inverse_area,
    edge_length,
    wet_mask,
    partner,
    volume_matrix,
    flux_in,
    flux_out,
    rows,
):
    element_count = state.shape[1]
    channels = rows.shape[0] // 3
    flat_traces = take_traces(state, rows)
    trace_table = jnp.concatenate([flat_traces, received.reshape(channels, -1)], axis=1)
    outer_traces = trace_table[:, partner.reshape(-1)].reshape(channels, 3, element_count)
    inner_traces = flat_traces.reshape(channels, 3, element_count)
    surf_inner = inner_traces[:8]
    surf_outer = outer_traces[:8]
    flux_surface = (
        jnp.einsum("ab,bfe->afe", flux_in, surf_inner, precision=lax.Precision.HIGHEST)
        - jnp.einsum("ab,bfe->afe", flux_out, surf_outer, precision=lax.Precision.HIGHEST)
        + 0.5 * wave_speed[None] * (surf_inner - surf_outer)
    )
    flux_pore = LATERAL * conductivity[None, None] * (outer_traces[8:] - inner_traces[8:])
    flux_all = jnp.concatenate([flux_surface, flux_pore], axis=0) * edge_length[None]
    lifted = lift_back(flux_all.reshape(channels * 3, element_count), rows, state.shape[0])
    volume = jnp.dot(volume_matrix, state[:12], precision=lax.Precision.HIGHEST)
    top_exchange = conductivity[None] * (state[9:12] - state[12:15])
    momentum = jnp.asarray(MOMENTUM_ROWS, dtype=jnp.float32)[:, None]
    surface = inverse_area[None] * (volume + lifted[:12]) - momentum * friction[None] * state[:12]
    surface = (
        jnp.concatenate([surface[:9], surface[9:12] - SALT_RETURN * top_exchange], axis=0)
        * wet_mask[None]
    )
    layers = state[12:].reshape(LAYERS, 3, element_count)
    between = conductivity[None, None] * (layers[:-1] - layers[1:])
    from_above = jnp.concatenate([top_exchange[None], between], axis=0)
    to_below = jnp.concatenate([between, jnp.zeros((1, 3, element_count), jnp.float32)], axis=0)
    pore = (from_above - to_below).reshape(3 * LAYERS, element_count) + inverse_area[None] * lifted[
        12:
    ]
    return jnp.concatenate([surface, pore], axis=0)


def forward_estuary(block, by_count):
    return shifted(block, "gx", by_count)


def forward_across(block, by_count):
    return shifted(block, "gy", by_count)


def backward_estuary(block, by_count):
    return shifted(block, "gx", by_count)


def backward_across(block, by_count):
    return shifted(block, "gy", by_count)


def route_blocks(blocks, estuary_hop, across_hop):
    pieces = [
        across_hop(estuary_hop(blocks[..., 7, :], 1), 1),
        estuary_hop(blocks[..., 6, :], 1),
        across_hop(estuary_hop(blocks[..., 5, :], 1), -1),
        across_hop(blocks[..., 4, :], 1),
        across_hop(blocks[..., 3, :], -1),
        across_hop(estuary_hop(blocks[..., 2, :], -1), 1),
        estuary_hop(blocks[..., 1, :], -1),
        across_hop(estuary_hop(blocks[..., 0, :], -1), -1),
    ]
    return jnp.stack(pieces, axis=-2)


def local(
    cotangent,
    section_states,
    inverse_area,
    edge_length,
    roughness,
    soil_conductance,
    zone_friction,
    zone_conductivity,
    wet_mask,
    element_zone,
    send_face,
    send_count,
    face_partner,
    volume_matrix,
    flux_in,
    flux_out,
):
    rows = jnp.asarray(trace_rows(), dtype=jnp.int32)
    channels = rows.shape[0] // 3
    cotangent_local = cotangent[0, 0]
    row_count = cotangent_local.shape[0]
    element_count = cotangent_local.shape[1]
    area_local = inverse_area[0, 0]
    edges_local = edge_length[0, 0]
    rough_local = roughness[0, 0]
    conduct_local = soil_conductance[0, 0]
    wetness = wet_mask[0, 0].astype(jnp.float32)
    zones_local = element_zone[0, 0]
    faces_sent = send_face[0, 0]
    counts_sent = send_count[0, 0]
    partner = face_partner[0, 0]
    zone_total = zone_friction.shape[0]
    conductivity = zone_conductivity[zones_local] * conduct_local
    zone_factor = zone_friction[zones_local]
    slot_index = jnp.arange(faces_sent.shape[1])
    live_slots = (slot_index[None, :] < counts_sent[:, None]).astype(jnp.float32)
    device_number = lax.axis_index("gx") * lax.axis_size("gy") + lax.axis_index("gy")
    zone_base = device_number * ZONE_DEV
    near_count = 2 * ZONE_DEV
    offset_zone = (zones_local - zone_base) % zone_total
    near_onehot = (offset_zone[None, :] == jnp.arange(near_count, dtype=jnp.int32)[:, None]).astype(
        jnp.float32
    )
    near_ids = (zone_base + jnp.arange(near_count, dtype=jnp.int32)) % zone_total
    forward_all = section_states[:, 0, 0].astype(jnp.float32)

    def section_received(states):
        flat_states = jax.vmap(lambda one: take_traces(one, rows))(states)
        outgoing = (flat_states[:, :, faces_sent] * live_slots[None, None]).astype(jnp.bfloat16)
        return route_blocks(outgoing, forward_estuary, forward_across).astype(jnp.float32)

    def received_of(section_no):
        return section_received(forward_all[section_no : section_no + 1])[0]

    def section_adjoint(section_no, weight_field):
        forward_state = forward_all[section_no]
        flat_forward = take_traces(forward_state, rows)
        received = received_of(section_no)
        trace_table = jnp.concatenate([flat_forward, received.reshape(channels, -1)], axis=1)
        outer_forward = trace_table[:, partner.reshape(-1)]
        wave_speed = section_speed(flat_forward, outer_forward).reshape(3, element_count)
        moment = jnp.sqrt(1.0 + jnp.mean(forward_state[3:9] ** 2, axis=0))
        friction_base = rough_local * moment
        friction = zone_factor * friction_base

        def section_operator(state, incoming, conduct_in, friction_in):
            return local_operator(
                state,
                incoming,
                conduct_in,
                friction_in,
                wave_speed,
                area_local,
                edges_local,
                wetness,
                partner,
                volume_matrix,
                flux_in,
                flux_out,
                rows,
            )

        unused, pullback = jax.vjp(
            section_operator, forward_state, received, conductivity, friction
        )
        state_bar, received_bar, conduct_bar, friction_bar = pullback(TIME_STEP * weight_field)
        returned = route_blocks(received_bar, backward_estuary, backward_across)
        flat_bar = (
            jnp.zeros((channels, 3 * element_count), jnp.float32)
            .at[:, faces_sent]
            .add(returned * live_slots[None])
        )
        state_bar = state_bar + lift_back(
            flat_bar.reshape(channels * 3, element_count), rows, row_count
        )
        element_terms = jnp.stack(
            [friction_base * friction_bar, conduct_local * conduct_bar], axis=0
        )
        near_terms = jnp.einsum(
            "ke,ze->kz", element_terms, near_onehot, precision=lax.Precision.HIGHEST
        )
        zone_terms = jnp.zeros((2, zone_total), jnp.float32).at[:, near_ids].add(near_terms)
        return (state_bar, zone_terms)

    bar_two, terms_two = section_adjoint(2, cotangent_local)
    lam_two = 2.0 / 3.0 * (cotangent_local + bar_two)
    bar_one, terms_one = section_adjoint(1, lam_two)
    lam_one = 0.25 * (lam_two + bar_one)
    bar_zero, terms_zero = section_adjoint(0, lam_one)
    adjoint = cotangent_local / 3.0 + 0.75 * lam_two + lam_one + bar_zero
    summed = [lax.psum(terms, ("gx", "gy")) for terms in (terms_two, terms_one, terms_zero)]
    zone_grads = GRAD_WEIGHT * (2.0 / 3.0 * summed[0] + 0.25 * summed[1] + summed[2])
    return (adjoint[None, None], zone_grads)


def solution(mesh):
    placed = (
        P("gx", "gy", None, None),
        P(None, "gx", "gy", None, None),
        P("gx", "gy", None),
        P("gx", "gy", None, None),
        P("gx", "gy", None),
        P("gx", "gy", None),
        P(),
        P(),
        P("gx", "gy", None),
        P("gx", "gy", None),
        P("gx", "gy", None, None),
        P("gx", "gy", None),
        P("gx", "gy", None, None),
        P(),
        P(),
        P(),
    )
    return jax.shard_map(
        local,
        mesh=mesh,
        in_specs=placed,
        out_specs=(P("gx", "gy", None, None), P()),
        check_vma=False,
    )
```

profile of v0, /device:TPU:41, one launch (start us, length us, event | category | flops | bytes accessed | tf_op | source)
XLA Modules:
  0.0 641.6 jit_solution(15260128408146421137)
XLA Ops:
  5.4 7.6 %gather_fusion.12 = f32[2048,28]{1,0:T(8,128)} fusion(f32[28,3072]{0,1:T(8,128)S(1)} %copy.369, s32[2048]{0:T(1024)S(1)} %broadcast_clamp_fusion.1), kind=kCustom, calls=%fused_computation.15 | custom fusion | bytes 466944 | tf_op jit(solution)/shard_map/gather | solution.py:177
  17.5 7.6 %gather_fusion.8 = f32[2048,28]{1,0:T(8,128)} fusion(f32[28,3072]{0,1:T(8,128)S(1)} %copy.340, s32[2048]{0:T(1024)S(1)} %broadcast_clamp_fusion.1), kind=kCustom, calls=%fused_computation.10 | custom fusion | bytes 466944 | tf_op jit(solution)/shard_map/gather | solution.py:177
  29.0 7.6 %gather_fusion.4 = f32[2048,28]{1,0:T(8,128)} fusion(f32[28,3072]{0,1:T(8,128)S(1)} %copy.311, s32[2048]{0:T(1024)S(1)} %broadcast_clamp_fusion.1), kind=kCustom, calls=%fused_computation.5 | custom fusion | bytes 466944 | tf_op jit(solution)/shard_map/gather | solution.py:177
  49.9 4.6 collective-permute-start.5
  59.3 6.9 %gather_fusion = f32[1024]{0:T(1024)S(1)} fusion(f32[512]{0:T(512)S(1)} %copy-done.1, s32[1024]{0:T(1024)S(1)} %broadcast_clamp_fusion.2), kind=kCustom, calls=%fused_computation | custom fusion | bytes 12288 | tf_op jit(solution)/shard_map/gather | solution.py:161
  66.2 6.9 %gather_fusion.1 = f32[1024]{0:T(1024)S(1)} fusion(f32[512]{0:T(512)S(1)} %copy-done.2, s32[1024]{0:T(1024)S(1)} %broadcast_clamp_fusion.2), kind=kCustom, calls=%fused_computation.1 | custom fusion | bytes 12288 | tf_op jit(solution)/shard_map/gather | solution.py:162
  82.1 4.6 collective-permute-start.7
  94.7 4.8 collective-permute-start.29
  101.5 4.3 collective-permute-start.33
  113.6 5.8 collective-permute-start.57
  150.4 5.5 collective-permute-start.31
  162.7 4.5 collective-permute-start.25
  172.6 10.9 %gather_fusion.5 = f32[3072,28]{1,0:T(8,128)} fusion(f32[28,5120]{0,1:T(8,128)S(1)} %copy.321, s32[3072]{0:T(1024)S(1)} %copy-done.60), kind=kCustom, calls=%fused_computation.6 | custom fusion | bytes 700416 | tf_op jit(solution)/shard_map/gather | solution.py:188
  190.1 17.9 %scatter_custom_fusion = f32[28,5120]{0,1:T(8,128)S(1)} fusion(s32[3072]{0:T(1024)} %bitcast.397, f32[3072,28]{1,0:T(8,128)} %copy.327, f32[]{:T(128)} %constant.38.clone.1), kind=kCustom, calls=%fused_computation.36 | custom fusion | flops 86016 | bytes 573952 | tf_op jit(solution)/shard_map/transpose(jvp())/scatter-add | solution.py:68
  211.8 5.5 collective-permute-start.55
  220.7 4.5 collective-permute-start.32
  249.4 11.9 %gather_fusion.9 = f32[3072,28]{1,0:T(8,128)} fusion(f32[28,5120]{0,1:T(8,128)S(1)} %copy.350, s32[3072]{0:T(1024)} %broadcast_clamp_fusion), kind=kCustom, calls=%fused_computation.11 | custom fusion | bytes 700416 | tf_op jit(solution)/shard_map/gather | solution.py:188
  273.2 4.5 collective-permute-start.17
  284.4 11.9 %gather_fusion.13 = f32[3072,28]{1,0:T(8,128)} fusion(f32[28,5120]{0,1:T(8,128)S(1)} %copy.379, s32[3072]{0:T(1024)} %broadcast_clamp_fusion), kind=kCustom, calls=%fused_computation.16 | custom fusion | bytes 700416 | tf_op jit(solution)/shard_map/gather | solution.py:188
  298.6 4.2 collective-permute-start.19
  310.5 4.5 collective-permute-start.13
  336.6 13.9 %scatter_custom_fusion.2 = f32[28,3072]{0,1:T(8,128)S(1)} fusion(s32[2048]{0:T(1024)} %bitcast.407, f32[2048,28]{1,0:T(8,128)} %bitcast.370, f32[]{:T(128)} %constant.38.clone.1), kind=kCustom, calls=%fused_computation.57 | custom fusion | flops 57344 | bytes 344576 | tf_op jit(solution)/shard_map/scatter-add | solution.py:219
  363.1 17.9 %scatter_custom_fusion.4 = f32[28,5120]{0,1:T(8,128)S(1)} fusion(s32[3072]{0:T(1024)} %bitcast.398, f32[3072,28]{1,0:T(8,128)} %copy.356, f32[]{:T(128)} %constant.38.clone.1), kind=kCustom, calls=%fused_computation.34 | custom fusion | flops 86016 | bytes 573952 | tf_op jit(solution)/shard_map/transpose(jvp())/scatter-add | solution.py:68
  395.5 4.4 collective-permute-start.41
  410.2 4.2 collective-permute-start.43
  424.2 4.5 collective-permute-start.37
  448.8 13.6 %scatter_custom_fusion.6 = f32[28,3072]{0,1:T(8,128)S(1)} fusion(s32[2048]{0:T(1024)} %bitcast.408, f32[2048,28]{1,0:T(8,128)S(1)} %bitcast.371, f32[]{:T(128)} %constant.38.clone.1), kind=kCustom, calls=%fused_computation.55 | custom fusion | flops 57344 | bytes 344576 | tf_op jit(solution)/shard_map/scatter-add | solution.py:219
  474.9 17.9 %scatter_custom_fusion.8 = f32[28,5120]{0,1:T(8,128)S(1)} fusion(s32[3072]{0:T(1024)} %bitcast.399, f32[3072,28]{1,0:T(8,128)} %copy.385, f32[]{:T(128)} %constant.38.clone.1), kind=kCustom, calls=%fused_computation.32 | custom fusion | flops 86016 | bytes 573952 | tf_op jit(solution)/shard_map/transpose(jvp())/scatter-add | solution.py:68
  506.3 4.4 collective-permute-start.65
  518.1 69.9 %all-reduce.42 = (f32[2,512]{0,1:T(8,128)}, f32[2,512]{0,1:T(8,128)}, f32[2,512]{0,1:T(8,128)}) all-reduce(f32[2,512]{0,1:T(8,128)S(1)} %scatter_custom_fusion.14, f32[2,512]{0,1:T(8,128)S(1)} %scatter_custom_fusion.13, f32[2,512]{0,1:T(8,128)} %scatter_custom_fusion.12), channel_id=1, replica_groups=mesh['gx'=16,'gy'=8] {'gx','gy'}, use_global_device_ids=true, to_apply=%region_35.36 | all-reduce | flops 3072 | bytes 24576 | tf_op jit(solution)/shard_map/psum | solution.py:239
  593.3 4.3 collective-permute-start.67
  624.9 13.6 %scatter_custom_fusion.10 = f32[28,3072]{0,1:T(8,128)S(1)} fusion(s32[2048]{0:T(1024)} %bitcast.409, f32[2048,28]{1,0:T(8,128)S(1)} %bitcast.369, f32[]{:T(128)} %constant.38.clone.1), kind=kCustom, calls=%fused_computation.53 | custom fusion | flops 57344 | bytes 344576 | tf_op jit(solution)/shard_map/scatter-add | solution.py:219
  (724 shorter events, 322.0 us)
Async XLA Ops:
  40.8 41.3 %collective-permute-start = (bf16[1,28,256]{2,1,0:T(8,128)(2,1)}, bf16[1,28,256]{2,1,0:T(8,128)(2,1)}, u32[]{:S(2)}, u32[]{:S(2)}) collective-permute-start(bf16[1,28,256]{2,1,0:T(8,128)(2,1)} %get-tuple-element.115), channel_id=1, source_target_pairs={{0,8},{8,16},{16,24},{24,32},{32,40},{40,48},{48,56},{56,64},{64,7... | collective-permute-start | bytes 43016 | tf_op jit(solution)/shard_map/ppermute | solution.py:20
  43.9 42.7 %collective-permute-start.2 = (bf16[1,28,256]{2,1,0:T(8,128)(2,1)}, bf16[1,28,256]{2,1,0:T(8,128)(2,1)}, u32[]{:S(2)}, u32[]{:S(2)}) collective-permute-start(bf16[1,28,256]{2,1,0:T(8,128)(2,1)} %get-tuple-element.114), channel_id=1, source_target_pairs={{0,8},{8,16},{16,24},{24,32},{32,40},{40,48},{48,56},{56,64},{64,7... | collective-permute-start | bytes 43016 | tf_op jit(solution)/shard_map/ppermute | solution.py:20
  47.0 42.4 %collective-permute-start.3 = (bf16[1,28,256]{2,1,0:T(8,128)(2,1)}, bf16[1,28,256]{2,1,0:T(8,128)(2,1)}, u32[]{:S(2)}, u32[]{:S(2)}) collective-permute-start(bf16[1,28,256]{2,1,0:T(8,128)(2,1)} %get-tuple-element.113), channel_id=1, source_target_pairs={{0,8},{8,16},{16,24},{24,32},{32,40},{40,48},{48,56},{56,64},{64,7... | collective-permute-start | bytes 43016 | tf_op jit(solution)/shard_map/ppermute | solution.py:20
  49.9 41.7 %collective-permute-start.5 = (bf16[1,28,256]{2,1,0:T(8,128)(2,1)}, bf16[1,28,256]{2,1,0:T(8,128)(2,1)}, u32[]{:S(2)}, u32[]{:S(2)}) collective-permute-start(bf16[1,28,256]{2,1,0:T(8,128)(2,1)} %get-tuple-element.112), channel_id=1, source_target_pairs={{0,1},{1,2},{2,3},{3,4},{4,5},{5,6},{6,7},{8,9},{9,10},{10,11},{11... | collective-permute-start | bytes 43016 | tf_op jit(solution)/shard_map/ppermute | solution.py:20
  54.5 40.3 %collective-permute-start.6 = (bf16[1,28,256]{2,1,0:T(8,128)(2,1)}, bf16[1,28,256]{2,1,0:T(8,128)(2,1)}, u32[]{:S(2)}, u32[]{:S(2)}) collective-permute-start(bf16[1,28,256]{2,1,0:T(8,128)(2,1)} %get-tuple-element.111), channel_id=1, source_target_pairs={{1,0},{2,1},{3,2},{4,3},{5,4},{6,5},{7,6},{9,8},{10,9},{11,10},{12... | collective-permute-start | bytes 43016 | tf_op jit(solution)/shard_map/ppermute | solution.py:20
  124.0 36.8 %collective-permute-start.24 = (bf16[1,28,256]{2,1,0:T(8,128)(2,1)S(1)}, bf16[1,28,256]{2,1,0:T(8,128)(2,1)}, u32[]{:S(2)}, u32[]{:S(2)}) collective-permute-start(bf16[1,28,256]{2,1,0:T(8,128)(2,1)S(1)} %get-tuple-element.107), channel_id=1, source_target_pairs={{0,8},{8,16},{16,24},{24,32},{32,40},{40,48},{48,56},{56,64},{64,7... | collective-permute-start | bytes 43016 | tf_op jit(solution)/shard_map/ppermute | solution.py:20
  125.9 36.8 %collective-permute-start.27 = (bf16[1,28,256]{2,1,0:T(8,128)(2,1)S(1)}, bf16[1,28,256]{2,1,0:T(8,128)(2,1)}, u32[]{:S(2)}, u32[]{:S(2)}) collective-permute-start(bf16[1,28,256]{2,1,0:T(8,128)(2,1)S(1)} %get-tuple-element.105), channel_id=1, source_target_pairs={{0,8},{8,16},{16,24},{24,32},{32,40},{40,48},{48,56},{56,64},{64,7... | collective-permute-start | bytes 43016 | tf_op jit(solution)/shard_map/ppermute | solution.py:20
  129.8 26.8 %collective-permute-start.8 = (bf16[1,28,256]{2,1,0:T(8,128)(2,1)}, bf16[1,28,256]{2,1,0:T(8,128)(2,1)}, u32[]{:S(2)}, u32[]{:S(2)}) collective-permute-start(bf16[1,28,256]{2,1,0:T(8,128)(2,1)} %collective-permute-done.7), channel_id=1, source_target_pairs={{0,1},{1,2},{2,3},{3,4},{4,5},{5,6},{6,7},{8,9},{9,10},{10,11},{11... | collective-permute-start | bytes 43016 | tf_op jit(solution)/shard_map/ppermute | solution.py:20
  133.5 33.7 %collective-permute-start.11 = (bf16[1,28,256]{2,1,0:T(8,128)(2,1)}, bf16[1,28,256]{2,1,0:T(8,128)(2,1)S(1)}, u32[]{:S(2)}, u32[]{:S(2)}) collective-permute-start(bf16[1,28,256]{2,1,0:T(8,128)(2,1)} %collective-permute-done.10), channel_id=1, source_target_pairs={{1,0},{2,1},{3,2},{4,3},{5,4},{6,5},{7,6},{9,8},{10,9},{11,10},{12... | collective-permute-start | bytes 43016 | tf_op jit(solution)/shard_map/ppermute | solution.py:20
  150.4 59.4 %collective-permute-start.31 = (bf16[1,28,256]{2,1,0:T(8,128)(2,1)}, bf16[1,28,256]{2,1,0:T(8,128)(2,1)}, u32[]{:S(2)}, u32[]{:S(2)}) collective-permute-start(bf16[1,28,256]{2,1,0:T(8,128)(2,1)} %get-tuple-element.102), channel_id=1, source_target_pairs={{8,0},{16,8},{24,16},{32,24},{40,32},{48,40},{56,48},{64,56},{72,6... | collective-permute-start | bytes 43016 | tf_op jit(solution)/shard_map/ppermute | solution.py:20
  156.6 55.2 %collective-permute-start.34 = (bf16[1,28,256]{2,1,0:T(8,128)(2,1)}, bf16[1,28,256]{2,1,0:T(8,128)(2,1)}, u32[]{:S(2)}, u32[]{:S(2)}) collective-permute-start(bf16[1,28,256]{2,1,0:T(8,128)(2,1)} %get-tuple-element.100), channel_id=1, source_target_pairs={{8,0},{16,8},{24,16},{32,24},{40,32},{48,40},{56,48},{64,56},{72,6... | collective-permute-start | bytes 43016 | tf_op jit(solution)/shard_map/ppermute | solution.py:20
  160.8 56.6 %collective-permute-start.48 = (bf16[1,28,256]{2,1,0:T(8,128)(2,1)}, bf16[1,28,256]{2,1,0:T(8,128)(2,1)}, u32[]{:S(2)}, u32[]{:S(2)}) collective-permute-start(bf16[1,28,256]{2,1,0:T(8,128)(2,1)} %get-tuple-element.99), channel_id=1, source_target_pairs={{0,8},{8,16},{16,24},{24,32},{32,40},{40,48},{48,56},{56,64},{64,7... | collective-permute-start | bytes 43016 | tf_op jit(solution)/shard_map/ppermute | solution.py:20
  162.7 58.0 %collective-permute-start.25 = (bf16[1,28,256]{2,1,0:T(8,128)(2,1)}, bf16[1,28,256]{2,1,0:T(8,128)(2,1)}, u32[]{:S(2)}, u32[]{:S(2)}) collective-permute-start(bf16[1,28,256]{2,1,0:T(8,128)(2,1)} %collective-permute-done.24), channel_id=1, source_target_pairs={{0,1},{1,2},{2,3},{3,4},{4,5},{5,6},{6,7},{8,9},{9,10},{10,11},{11... | collective-permute-start | bytes 43016 | tf_op jit(solution)/shard_map/ppermute | solution.py:20
  167.2 58.0 %collective-permute-start.28 = (bf16[1,28,256]{2,1,0:T(8,128)(2,1)}, bf16[1,28,256]{2,1,0:T(8,128)(2,1)}, u32[]{:S(2)}, u32[]{:S(2)}) collective-permute-start(bf16[1,28,256]{2,1,0:T(8,128)(2,1)} %collective-permute-done.27), channel_id=1, source_target_pairs={{1,0},{2,1},{3,2},{4,3},{5,4},{6,5},{7,6},{9,8},{10,9},{11,10},{12... | collective-permute-start | bytes 43016 | tf_op jit(solution)/shard_map/ppermute | solution.py:20
  232.1 34.7 %collective-permute-start.49 = (bf16[1,28,256]{2,1,0:T(8,128)(2,1)}, bf16[1,28,256]{2,1,0:T(8,128)(2,1)}, u32[]{:S(2)}, u32[]{:S(2)}) collective-permute-start(bf16[1,28,256]{2,1,0:T(8,128)(2,1)} %collective-permute-done.48), channel_id=1, source_target_pairs={{0,1},{1,2},{2,3},{3,4},{4,5},{5,6},{6,7},{8,9},{9,10},{10,11},{11... | collective-permute-start | bytes 43016 | tf_op jit(solution)/shard_map/ppermute | solution.py:20
  235.8 33.7 %collective-permute-start.52 = (bf16[1,28,256]{2,1,0:T(8,128)(2,1)}, bf16[1,28,256]{2,1,0:T(8,128)(2,1)}, u32[]{:S(2)}, u32[]{:S(2)}) collective-permute-start(bf16[1,28,256]{2,1,0:T(8,128)(2,1)} %collective-permute-done.51), channel_id=1, source_target_pairs={{1,0},{2,1},{3,2},{4,3},{5,4},{6,5},{7,6},{9,8},{10,9},{11,10},{12... | collective-permute-start | bytes 43016 | tf_op jit(solution)/shard_map/ppermute | solution.py:20
  237.7 35.4 %collective-permute-start.56 = (bf16[1,28,256]{2,1,0:T(8,128)(2,1)}, bf16[1,28,256]{2,1,0:T(8,128)(2,1)}, u32[]{:S(2)}, u32[]{:S(2)}) collective-permute-start(bf16[1,28,256]{2,1,0:T(8,128)(2,1)} %collective-permute-done.55), channel_id=1, source_target_pairs={{0,1},{1,2},{2,3},{3,4},{4,5},{5,6},{6,7},{8,9},{9,10},{10,11},{11... | collective-permute-start | bytes 43016 | tf_op jit(solution)/shard_map/ppermute | solution.py:20
  241.4 37.0 %collective-permute-start.59 = (bf16[1,28,256]{2,1,0:T(8,128)(2,1)}, bf16[1,28,256]{2,1,0:T(8,128)(2,1)}, u32[]{:S(2)}, u32[]{:S(2)}) collective-permute-start(bf16[1,28,256]{2,1,0:T(8,128)(2,1)} %collective-permute-done.58), channel_id=1, source_target_pairs={{1,0},{2,1},{3,2},{4,3},{5,4},{6,5},{7,6},{9,8},{10,9},{11,10},{12... | collective-permute-start | bytes 43016 | tf_op jit(solution)/shard_map/ppermute | solution.py:20
  243.4 55.2 %collective-permute-start.12 = (f32[28,256]{1,0:T(8,128)}, f32[28,256]{1,0:T(8,128)}, u32[]{:S(2)}, u32[]{:S(2)}) collective-permute-start(f32[28,256]{1,0:T(8,128)} %bitcast.43), channel_id=1, source_target_pairs={{0,8},{8,16},{16,24},{24,32},{32,40},{40,48},{48,56},{56,64},{64,7... | collective-permute-start | bytes 86024 | tf_op jit(solution)/shard_map/ppermute | solution.py:20
  266.8 35.9 %collective-permute-start.14 = (f32[28,256]{1,0:T(8,128)}, f32[28,256]{1,0:T(8,128)}, u32[]{:S(2)}, u32[]{:S(2)}) collective-permute-start(f32[28,256]{1,0:T(8,128)} %bitcast.44), channel_id=1, source_target_pairs={{0,8},{8,16},{16,24},{24,32},{32,40},{40,48},{48,56},{56,64},{64,7... | collective-permute-start | bytes 86024 | tf_op jit(solution)/shard_map/ppermute | solution.py:20
  269.5 37.7 %collective-permute-start.15 = (f32[28,256]{1,0:T(8,128)}, f32[28,256]{1,0:T(8,128)}, u32[]{:S(2)}, u32[]{:S(2)}) collective-permute-start(f32[28,256]{1,0:T(8,128)} %bitcast.45), channel_id=1, source_target_pairs={{0,8},{8,16},{16,24},{24,32},{32,40},{40,48},{48,56},{56,64},{64,7... | collective-permute-start | bytes 86024 | tf_op jit(solution)/shard_map/ppermute | solution.py:20
  273.2 37.3 %collective-permute-start.17 = (f32[28,256]{1,0:T(8,128)}, f32[28,256]{1,0:T(8,128)}, u32[]{:S(2)}, u32[]{:S(2)}) collective-permute-start(f32[28,256]{1,0:T(8,128)} %bitcast.46), channel_id=1, source_target_pairs={{0,1},{1,2},{2,3},{3,4},{4,5},{5,6},{6,7},{8,9},{9,10},{10,11},{11... | collective-permute-start | bytes 86024 | tf_op jit(solution)/shard_map/ppermute | solution.py:20
  278.4 36.6 %collective-permute-start.18 = (f32[28,256]{1,0:T(8,128)}, f32[28,256]{1,0:T(8,128)}, u32[]{:S(2)}, u32[]{:S(2)}) collective-permute-start(f32[28,256]{1,0:T(8,128)} %bitcast.47), channel_id=1, source_target_pairs={{1,0},{2,1},{3,2},{4,3},{5,4},{6,5},{7,6},{9,8},{10,9},{11,10},{12... | collective-permute-start | bytes 86024 | tf_op jit(solution)/shard_map/ppermute | solution.py:20
  387.4 27.0 %collective-permute-start.38 = (f32[28,256]{1,0:T(8,128)}, f32[28,256]{1,0:T(8,128)}, u32[]{:S(2)}, u32[]{:S(2)}) collective-permute-start(f32[28,256]{1,0:T(8,128)} %bitcast.82), channel_id=1, source_target_pairs={{0,8},{8,16},{16,24},{24,32},{32,40},{40,48},{48,56},{56,64},{64,7... | collective-permute-start | bytes 86024 | tf_op jit(solution)/shard_map/ppermute | solution.py:20
  390.9 30.0 %collective-permute-start.39 = (f32[28,256]{1,0:T(8,128)}, f32[28,256]{1,0:T(8,128)}, u32[]{:S(2)}, u32[]{:S(2)}) collective-permute-start(f32[28,256]{1,0:T(8,128)} %bitcast.83), channel_id=1, source_target_pairs={{0,8},{8,16},{16,24},{24,32},{32,40},{40,48},{48,56},{56,64},{64,7... | collective-permute-start | bytes 86024 | tf_op jit(solution)/shard_map/ppermute | solution.py:20
  395.5 28.7 %collective-permute-start.41 = (f32[28,256]{1,0:T(8,128)}, f32[28,256]{1,0:T(8,128)}, u32[]{:S(2)}, u32[]{:S(2)}) collective-permute-start(f32[28,256]{1,0:T(8,128)} %bitcast.84), channel_id=1, source_target_pairs={{0,1},{1,2},{2,3},{3,4},{4,5},{5,6},{6,7},{8,9},{9,10},{10,11},{11... | collective-permute-start | bytes 86024 | tf_op jit(solution)/shard_map/ppermute | solution.py:20
  400.9 27.8 %collective-permute-start.42 = (f32[28,256]{1,0:T(8,128)S(1)}, f32[28,256]{1,0:T(8,128)}, u32[]{:S(2)}, u32[]{:S(2)}) collective-permute-start(f32[28,256]{1,0:T(8,128)S(1)} %bitcast.403), channel_id=1, source_target_pairs={{1,0},{2,1},{3,2},{4,3},{5,4},{6,5},{7,6},{9,8},{10,9},{11,10},{12... | collective-permute-start | bytes 86024 | tf_op jit(solution)/shard_map/ppermute | solution.py:20
  495.6 97.7 %collective-permute-start.60 = (f32[28,256]{1,0:T(8,128)}, f32[28,256]{1,0:T(8,128)}, u32[]{:S(2)}, u32[]{:S(2)}) collective-permute-start(f32[28,256]{1,0:T(8,128)} %bitcast.119), channel_id=1, source_target_pairs={{0,8},{8,16},{16,24},{24,32},{32,40},{40,48},{48,56},{56,64},{64,7... | collective-permute-start | bytes 86024 | tf_op jit(solution)/shard_map/ppermute | solution.py:20
  499.2 98.4 %collective-permute-start.62 = (f32[28,256]{1,0:T(8,128)}, f32[28,256]{1,0:T(8,128)}, u32[]{:S(2)}, u32[]{:S(2)}) collective-permute-start(f32[28,256]{1,0:T(8,128)} %bitcast.120), channel_id=1, source_target_pairs={{0,8},{8,16},{16,24},{24,32},{32,40},{40,48},{48,56},{56,64},{64,7... | collective-permute-start | bytes 86024 | tf_op jit(solution)/shard_map/ppermute | solution.py:20
  502.7 99.3 %collective-permute-start.63 = (f32[28,256]{1,0:T(8,128)}, f32[28,256]{1,0:T(8,128)}, u32[]{:S(2)}, u32[]{:S(2)}) collective-permute-start(f32[28,256]{1,0:T(8,128)} %bitcast.121), channel_id=1, source_target_pairs={{0,8},{8,16},{16,24},{24,32},{32,40},{40,48},{48,56},{56,64},{64,7... | collective-permute-start | bytes 86024 | tf_op jit(solution)/shard_map/ppermute | solution.py:20
  506.3 98.4 %collective-permute-start.65 = (f32[28,256]{1,0:T(8,128)}, f32[28,256]{1,0:T(8,128)}, u32[]{:S(2)}, u32[]{:S(2)}) collective-permute-start(f32[28,256]{1,0:T(8,128)} %bitcast.122), channel_id=1, source_target_pairs={{0,1},{1,2},{2,3},{3,4},{4,5},{5,6},{6,7},{8,9},{9,10},{10,11},{11... | collective-permute-start | bytes 86024 | tf_op jit(solution)/shard_map/ppermute | solution.py:20
  510.8 97.0 %collective-permute-start.66 = (f32[28,256]{1,0:T(8,128)S(1)}, f32[28,256]{1,0:T(8,128)}, u32[]{:S(2)}, u32[]{:S(2)}) collective-permute-start(f32[28,256]{1,0:T(8,128)S(1)} %bitcast.402), channel_id=1, source_target_pairs={{1,0},{2,1},{3,2},{4,3},{5,4},{6,5},{7,6},{9,8},{10,9},{11,10},{12... | collective-permute-start | bytes 86024 | tf_op jit(solution)/shard_map/ppermute | solution.py:20
  (193 other events, 2815.2 us)
where the time goes:
time: 654 us; the launch traced here: 642 us
  starting transfers between devices  219 us (33%)
  local copies, waits for them, and re-layouts  197 us (30%)
  other arithmetic  143 us (22%)
  blocking collectives  69.9 us (11%)
  matrix products  7.69 us (1%)
    ppermute x72, starting transfers between devices, shifted(): return lax.ppermute(x, axis, pairs)  219 us
    psum x1, blocking collectives, local(): lax.psum(terms, ('gx', 'gy'))  69.9 us
    scatter-add x3, other arithmetic, local_operator(): trace_table[:, partner.reshape(-1)].reshape(channels, 3, element_count)  53.6 us
    scatter-add x3, other arithmetic, section_adjoint(): flat_bar = jnp.zeros((channels, 3 * element_count), jnp.float32).at[:, fa...  41.2 us
    gather x6, local copies, waits for them, and re-layouts, section_adjoint(): outer_forward = trace_table[:, partner.reshape(-1)]  40.6 us
    unnamed x343, local copies, waits for them, and re-layouts  36.6 us
    gather x6, local copies, waits for them, and re-layouts, section_received(): flat_states[:, :, faces_sent] * live_slots[None, None]  29 us
    another operation x54, local copies, waits for them, and re-layouts, route_blocks(): return jnp.stack(pieces, axis=-2)  28.7 us
  transfers between devices with their start and end apart: 72, of which 0 were waited for; matrix products, arithmetic and copies ran while one was open for 29% of the time, Pallas kernels for 0%

commit v1 on v0

--- a/solution.py
+++ b/solution.py
@@ -236,7 +236,7 @@
     lam_one = 0.25 * (lam_two + bar_one)
     bar_zero, terms_zero = section_adjoint(0, lam_one)
     adjoint = cotangent_local / 3.0 + 0.75 * lam_two + lam_one + bar_zero
-    summed = [lax.psum(terms, ("gx", "gy")) for terms in (terms_two, terms_one, terms_zero)]
+    summed = [lax.psum(lax.psum(terms, "gx"), "gy") for terms in (terms_two, terms_one, terms_zero)]
     zone_grads = GRAD_WEIGHT * (2.0 / 3.0 * summed[0] + 0.25 * summed[1] + summed[2])
     return (adjoint[None, None], zone_grads)
 

time: 654 us -> 694 us (1.061)
  the two profiles are of different devices: /device:TPU:41 before, /device:TPU:7 now
where the time goes in v1:
time: 694 us; the launch traced here: 682 us
  starting transfers between devices  228 us (33%)
  local copies, waits for them, and re-layouts  197 us (28%)
  other arithmetic  143 us (21%)
  blocking collectives  102 us (15%)
  matrix products  7.65 us (1%)
    ppermute x72, starting transfers between devices, shifted(): return lax.ppermute(x, axis, pairs)  228 us
    psum x1, blocking collectives, local(): lax.psum(terms, 'gx')  61 us
    scatter-add x3, other arithmetic, local_operator(): trace_table[:, partner.reshape(-1)].reshape(channels, 3, element_count)  53.6 us
    scatter-add x3, other arithmetic, section_adjoint(): flat_bar = jnp.zeros((channels, 3 * element_count), jnp.float32).at[:, fa...  41.1 us
    gather x6, local copies, waits for them, and re-layouts, section_adjoint(): outer_forward = trace_table[:, partner.reshape(-1)]  40.7 us
    psum x1, blocking collectives, local(): lax.psum(lax.psum(terms, 'gx'), 'gy')  40.6 us
    unnamed x343, local copies, waits for them, and re-layouts  36.5 us
    gather x6, local copies, waits for them, and re-layouts, section_received(): flat_states[:, :, faces_sent] * live_slots[None, None]  28.9 us
  transfers between devices with their start and end apart: 72, of which 0 were waited for; matrix products, arithmetic and copies ran while one was open for 27% of the time, Pallas kernels for 0%

profile of v1, /device:TPU:7, one launch (start us, length us, event | category | flops | bytes accessed | tf_op | source)
XLA Modules:
  0.0 682.0 jit_solution(12414442619728107310)
XLA Ops:
  5.4 7.6 %gather_fusion.12 = f32[2048,28]{1,0:T(8,128)} fusion(f32[28,3072]{0,1:T(8,128)S(1)} %copy.369, s32[2048]{0:T(1024)S(1)} %broadcast_clamp_fusion.1), kind=kCustom, calls=%fused_computation.15 | custom fusion | bytes 466944 | tf_op jit(solution)/shard_map/gather | solution.py:177
  17.5 7.6 %gather_fusion.8 = f32[2048,28]{1,0:T(8,128)} fusion(f32[28,3072]{0,1:T(8,128)S(1)} %copy.340, s32[2048]{0:T(1024)S(1)} %broadcast_clamp_fusion.1), kind=kCustom, calls=%fused_computation.10 | custom fusion | bytes 466944 | tf_op jit(solution)/shard_map/gather | solution.py:177
  29.0 7.6 %gather_fusion.4 = f32[2048,28]{1,0:T(8,128)} fusion(f32[28,3072]{0,1:T(8,128)S(1)} %copy.311, s32[2048]{0:T(1024)S(1)} %broadcast_clamp_fusion.1), kind=kCustom, calls=%fused_computation.5 | custom fusion | bytes 466944 | tf_op jit(solution)/shard_map/gather | solution.py:177
  50.5 4.6 collective-permute-start.5
  59.9 6.9 %gather_fusion = f32[1024]{0:T(1024)S(1)} fusion(f32[512]{0:T(512)S(1)} %copy-done.1, s32[1024]{0:T(1024)S(1)} %broadcast_clamp_fusion.2), kind=kCustom, calls=%fused_computation | custom fusion | bytes 12288 | tf_op jit(solution)/shard_map/gather | solution.py:161
  66.8 6.9 %gather_fusion.1 = f32[1024]{0:T(1024)S(1)} fusion(f32[512]{0:T(512)S(1)} %copy-done.2, s32[1024]{0:T(1024)S(1)} %broadcast_clamp_fusion.2), kind=kCustom, calls=%fused_computation.1 | custom fusion | bytes 12288 | tf_op jit(solution)/shard_map/gather | solution.py:162
  90.1 5.0 collective-permute-start.26
  95.1 4.8 collective-permute-start.29
  103.8 5.5 collective-permute-start.50
  109.3 4.2 collective-permute-start.53
  121.7 5.7 collective-permute-start.24
  158.7 5.5 collective-permute-start.48
  164.2 4.5 collective-permute-start.25
  174.1 10.9 %gather_fusion.5 = f32[3072,28]{1,0:T(8,128)} fusion(f32[28,5120]{0,1:T(8,128)S(1)} %copy.321, s32[3072]{0:T(1024)S(1)} %copy-done.60), kind=kCustom, calls=%fused_computation.6 | custom fusion | bytes 700416 | tf_op jit(solution)/shard_map/gather | solution.py:188
  191.6 17.9 %scatter_custom_fusion = f32[28,5120]{0,1:T(8,128)S(1)} fusion(s32[3072]{0:T(1024)} %bitcast.397, f32[3072,28]{1,0:T(8,128)} %copy.327, f32[]{:T(128)} %constant.38.clone.1), kind=kCustom, calls=%fused_computation.36 | custom fusion | flops 86016 | bytes 573952 | tf_op jit(solution)/shard_map/transpose(jvp())/scatter-add | solution.py:68
  241.0 5.8 collective-permute-start.12
  250.9 11.9 %gather_fusion.9 = f32[3072,28]{1,0:T(8,128)} fusion(f32[28,5120]{0,1:T(8,128)S(1)} %copy.350, s32[3072]{0:T(1024)} %broadcast_clamp_fusion), kind=kCustom, calls=%fused_computation.11 | custom fusion | bytes 700416 | tf_op jit(solution)/shard_map/gather | solution.py:188
  273.7 4.2 collective-permute-start.17
  284.6 11.9 %gather_fusion.13 = f32[3072,28]{1,0:T(8,128)} fusion(f32[28,5120]{0,1:T(8,128)S(1)} %copy.379, s32[3072]{0:T(1024)} %broadcast_clamp_fusion), kind=kCustom, calls=%fused_computation.16 | custom fusion | bytes 700416 | tf_op jit(solution)/shard_map/gather | solution.py:188
  308.5 4.2 collective-permute-start.13
  334.3 13.9 %scatter_custom_fusion.2 = f32[28,3072]{0,1:T(8,128)S(1)} fusion(s32[2048]{0:T(1024)} %bitcast.407, f32[2048,28]{1,0:T(8,128)} %bitcast.370, f32[]{:T(128)} %constant.38.clone.1), kind=kCustom, calls=%fused_computation.57 | custom fusion | flops 57344 | bytes 344576 | tf_op jit(solution)/shard_map/scatter-add | solution.py:219
  360.8 17.9 %scatter_custom_fusion.4 = f32[28,5120]{0,1:T(8,128)S(1)} fusion(s32[3072]{0:T(1024)} %bitcast.398, f32[3072,28]{1,0:T(8,128)} %copy.356, f32[]{:T(128)} %constant.38.clone.1), kind=kCustom, calls=%fused_computation.34 | custom fusion | flops 86016 | bytes 573952 | tf_op jit(solution)/shard_map/transpose(jvp())/scatter-add | solution.py:68
  381.5 5.7 collective-permute-start.36
  422.1 4.2 collective-permute-start.37
  446.3 13.6 %scatter_custom_fusion.6 = f32[28,3072]{0,1:T(8,128)S(1)} fusion(s32[2048]{0:T(1024)} %bitcast.408, f32[2048,28]{1,0:T(8,128)S(1)} %bitcast.371, f32[]{:T(128)} %constant.38.clone.1), kind=kCustom, calls=%fused_computation.55 | custom fusion | flops 57344 | bytes 344576 | tf_op jit(solution)/shard_map/scatter-add | solution.py:219
  472.5 17.9 %scatter_custom_fusion.8 = f32[28,5120]{0,1:T(8,128)S(1)} fusion(s32[3072]{0:T(1024)} %bitcast.399, f32[3072,28]{1,0:T(8,128)} %copy.385, f32[]{:T(128)} %constant.38.clone.1), kind=kCustom, calls=%fused_computation.32 | custom fusion | flops 86016 | bytes 573952 | tf_op jit(solution)/shard_map/transpose(jvp())/scatter-add | solution.py:68
  493.2 5.7 collective-permute-start.60
  518.5 61.0 %all-reduce.42 = (f32[2,512]{0,1:T(8,128)}, f32[2,512]{0,1:T(8,128)}, f32[2,512]{0,1:T(8,128)}) all-reduce(f32[2,512]{0,1:T(8,128)S(1)} %scatter_custom_fusion.14, f32[2,512]{0,1:T(8,128)S(1)} %scatter_custom_fusion.13, f32[2,512]{0,1:T(8,128)} %scatter_custom_fusion.12), channel_id=1, replica_groups=mesh['gx'=16,'gy'=8] {'gx'}, use_global_device_ids=true, to_apply=%region_37.38 | all-reduce | flops 3072 | bytes 24576 | tf_op jit(solution)/shard_map/psum | solution.py:239
  579.5 40.6 %all-reduce.43 = (f32[2,512]{0,1:T(8,128)S(1)}, f32[2,512]{0,1:T(8,128)}, f32[2,512]{0,1:T(8,128)}) all-reduce(f32[2,512]{0,1:T(8,128)} %get-tuple-element.21, f32[2,512]{0,1:T(8,128)} %get-tuple-element.22, f32[2,512]{0,1:T(8,128)} %get-tuple-element.23), channel_id=1, replica_groups=mesh['gx'=16,'gy'=8] {'gy'}, use_global_device_ids=true, to_apply=%region_38.39 | all-reduce | flops 3072 | bytes 24576 | tf_op jit(solution)/shard_map/psum | solution.py:239
  625.3 7.2 %collective-permute-start.67 = (f32[28,256]{1,0:T(8,128)}, f32[28,256]{1,0:T(8,128)}, u32[]{:S(2)}, u32[]{:S(2)}) collective-permute-start(f32[28,256]{1,0:T(8,128)} %bitcast.124), channel_id=1, source_target_pairs={{8,0},{16,8},{24,16},{32,24},{40,32},{48,40},{56,48},{64,56},{72,6... | collective-permute-start | bytes 86024 | tf_op jit(solution)/shard_map/ppermute | solution.py:20
  636.9 6.7 collective-permute-start.69
  665.2 13.6 %scatter_custom_fusion.10 = f32[28,3072]{0,1:T(8,128)S(1)} fusion(s32[2048]{0:T(1024)} %bitcast.409, f32[2048,28]{1,0:T(8,128)S(1)} %bitcast.369, f32[]{:T(128)} %constant.38.clone.1), kind=kCustom, calls=%fused_computation.53 | custom fusion | flops 57344 | bytes 344576 | tf_op jit(solution)/shard_map/scatter-add | solution.py:219
  (725 shorter events, 326.1 us)
Async XLA Ops:
  40.8 41.9 %collective-permute-start = (bf16[1,28,256]{2,1,0:T(8,128)(2,1)}, bf16[1,28,256]{2,1,0:T(8,128)(2,1)}, u32[]{:S(2)}, u32[]{:S(2)}) collective-permute-start(bf16[1,28,256]{2,1,0:T(8,128)(2,1)} %get-tuple-element.118), channel_id=1, source_target_pairs={{0,8},{8,16},{16,24},{24,32},{32,40},{40,48},{48,56},{56,64},{64,7... | collective-permute-start | bytes 43016 | tf_op jit(solution)/shard_map/ppermute | solution.py:20
  44.2 40.6 %collective-permute-start.2 = (bf16[1,28,256]{2,1,0:T(8,128)(2,1)}, bf16[1,28,256]{2,1,0:T(8,128)(2,1)}, u32[]{:S(2)}, u32[]{:S(2)}) collective-permute-start(bf16[1,28,256]{2,1,0:T(8,128)(2,1)} %get-tuple-element.117), channel_id=1, source_target_pairs={{0,8},{8,16},{16,24},{24,32},{32,40},{40,48},{48,56},{56,64},{64,7... | collective-permute-start | bytes 43016 | tf_op jit(solution)/shard_map/ppermute | solution.py:20
  47.4 40.3 %collective-permute-start.3 = (bf16[1,28,256]{2,1,0:T(8,128)(2,1)}, bf16[1,28,256]{2,1,0:T(8,128)(2,1)}, u32[]{:S(2)}, u32[]{:S(2)}) collective-permute-start(bf16[1,28,256]{2,1,0:T(8,128)(2,1)} %get-tuple-element.116), channel_id=1, source_target_pairs={{0,8},{8,16},{16,24},{24,32},{32,40},{40,48},{48,56},{56,64},{64,7... | collective-permute-start | bytes 43016 | tf_op jit(solution)/shard_map/ppermute | solution.py:20
  50.5 39.6 %collective-permute-start.5 = (bf16[1,28,256]{2,1,0:T(8,128)(2,1)}, bf16[1,28,256]{2,1,0:T(8,128)(2,1)}, u32[]{:S(2)}, u32[]{:S(2)}) collective-permute-start(bf16[1,28,256]{2,1,0:T(8,128)(2,1)} %get-tuple-element.115), channel_id=1, source_target_pairs={{0,1},{1,2},{2,3},{3,4},{4,5},{5,6},{6,7},{8,9},{9,10},{10,11},{11... | collective-permute-start | bytes 43016 | tf_op jit(solution)/shard_map/ppermute | solution.py:20
  55.1 40.0 %collective-permute-start.6 = (bf16[1,28,256]{2,1,0:T(8,128)(2,1)}, bf16[1,28,256]{2,1,0:T(8,128)(2,1)}, u32[]{:S(2)}, u32[]{:S(2)}) collective-permute-start(bf16[1,28,256]{2,1,0:T(8,128)(2,1)} %get-tuple-element.114), channel_id=1, source_target_pairs={{1,0},{2,1},{3,2},{4,3},{5,4},{6,5},{7,6},{9,8},{10,9},{11,10},{12... | collective-permute-start | bytes 43016 | tf_op jit(solution)/shard_map/ppermute | solution.py:20
  121.7 37.1 %collective-permute-start.24 = (bf16[1,28,256]{2,1,0:T(8,128)(2,1)S(1)}, bf16[1,28,256]{2,1,0:T(8,128)(2,1)}, u32[]{:S(2)}, u32[]{:S(2)}) collective-permute-start(bf16[1,28,256]{2,1,0:T(8,128)(2,1)S(1)} %get-tuple-element.110), channel_id=1, source_target_pairs={{0,8},{8,16},{16,24},{24,32},{32,40},{40,48},{48,56},{56,64},{64,7... | collective-permute-start | bytes 43016 | tf_op jit(solution)/shard_map/ppermute | solution.py:20
  127.4 36.8 %collective-permute-start.27 = (bf16[1,28,256]{2,1,0:T(8,128)(2,1)S(1)}, bf16[1,28,256]{2,1,0:T(8,128)(2,1)}, u32[]{:S(2)}, u32[]{:S(2)}) collective-permute-start(bf16[1,28,256]{2,1,0:T(8,128)(2,1)S(1)} %get-tuple-element.108), channel_id=1, source_target_pairs={{0,8},{8,16},{16,24},{24,32},{32,40},{40,48},{48,56},{56,64},{64,7... | collective-permute-start | bytes 43016 | tf_op jit(solution)/shard_map/ppermute | solution.py:20
  135.0 33.7 %collective-permute-start.11 = (bf16[1,28,256]{2,1,0:T(8,128)(2,1)}, bf16[1,28,256]{2,1,0:T(8,128)(2,1)S(1)}, u32[]{:S(2)}, u32[]{:S(2)}) collective-permute-start(bf16[1,28,256]{2,1,0:T(8,128)(2,1)} %collective-permute-done.10), channel_id=1, source_target_pairs={{1,0},{2,1},{3,2},{4,3},{5,4},{6,5},{7,6},{9,8},{10,9},{11,10},{12... | collective-permute-start | bytes 43016 | tf_op jit(solution)/shard_map/ppermute | solution.py:20
  151.9 59.4 %collective-permute-start.31 = (bf16[1,28,256]{2,1,0:T(8,128)(2,1)}, bf16[1,28,256]{2,1,0:T(8,128)(2,1)}, u32[]{:S(2)}, u32[]{:S(2)}) collective-permute-start(bf16[1,28,256]{2,1,0:T(8,128)(2,1)} %get-tuple-element.105), channel_id=1, source_target_pairs={{8,0},{16,8},{24,16},{32,24},{40,32},{48,40},{56,48},{64,56},{72,6... | collective-permute-start | bytes 43016 | tf_op jit(solution)/shard_map/ppermute | solution.py:20
  156.0 57.3 %collective-permute-start.34 = (bf16[1,28,256]{2,1,0:T(8,128)(2,1)}, bf16[1,28,256]{2,1,0:T(8,128)(2,1)}, u32[]{:S(2)}, u32[]{:S(2)}) collective-permute-start(bf16[1,28,256]{2,1,0:T(8,128)(2,1)} %get-tuple-element.103), channel_id=1, source_target_pairs={{8,0},{16,8},{24,16},{32,24},{40,32},{48,40},{56,48},{64,56},{72,6... | collective-permute-start | bytes 43016 | tf_op jit(solution)/shard_map/ppermute | solution.py:20
  158.7 58.0 %collective-permute-start.48 = (bf16[1,28,256]{2,1,0:T(8,128)(2,1)}, bf16[1,28,256]{2,1,0:T(8,128)(2,1)}, u32[]{:S(2)}, u32[]{:S(2)}) collective-permute-start(bf16[1,28,256]{2,1,0:T(8,128)(2,1)} %get-tuple-element.102), channel_id=1, source_target_pairs={{0,8},{8,16},{16,24},{24,32},{32,40},{40,48},{48,56},{56,64},{64,7... | collective-permute-start | bytes 43016 | tf_op jit(solution)/shard_map/ppermute | solution.py:20
  164.2 54.5 %collective-permute-start.25 = (bf16[1,28,256]{2,1,0:T(8,128)(2,1)}, bf16[1,28,256]{2,1,0:T(8,128)(2,1)}, u32[]{:S(2)}, u32[]{:S(2)}) collective-permute-start(bf16[1,28,256]{2,1,0:T(8,128)(2,1)} %collective-permute-done.24), channel_id=1, source_target_pairs={{0,1},{1,2},{2,3},{3,4},{4,5},{5,6},{6,7},{8,9},{9,10},{10,11},{11... | collective-permute-start | bytes 43016 | tf_op jit(solution)/shard_map/ppermute | solution.py:20
  168.7 54.2 %collective-permute-start.28 = (bf16[1,28,256]{2,1,0:T(8,128)(2,1)}, bf16[1,28,256]{2,1,0:T(8,128)(2,1)}, u32[]{:S(2)}, u32[]{:S(2)}) collective-permute-start(bf16[1,28,256]{2,1,0:T(8,128)(2,1)} %collective-permute-done.27), channel_id=1, source_target_pairs={{1,0},{2,1},{3,2},{4,3},{5,4},{6,5},{7,6},{9,8},{10,9},{11,10},{12... | collective-permute-start | bytes 43016 | tf_op jit(solution)/shard_map/ppermute | solution.py:20
  229.8 38.5 %collective-permute-start.49 = (bf16[1,28,256]{2,1,0:T(8,128)(2,1)}, bf16[1,28,256]{2,1,0:T(8,128)(2,1)}, u32[]{:S(2)}, u32[]{:S(2)}) collective-permute-start(bf16[1,28,256]{2,1,0:T(8,128)(2,1)} %collective-permute-done.48), channel_id=1, source_target_pairs={{0,1},{1,2},{2,3},{3,4},{4,5},{5,6},{6,7},{8,9},{9,10},{10,11},{11... | collective-permute-start | bytes 43016 | tf_op jit(solution)/shard_map/ppermute | solution.py:20
  233.5 37.5 %collective-permute-start.52 = (bf16[1,28,256]{2,1,0:T(8,128)(2,1)}, bf16[1,28,256]{2,1,0:T(8,128)(2,1)}, u32[]{:S(2)}, u32[]{:S(2)}) collective-permute-start(bf16[1,28,256]{2,1,0:T(8,128)(2,1)} %collective-permute-done.51), channel_id=1, source_target_pairs={{1,0},{2,1},{3,2},{4,3},{5,4},{6,5},{7,6},{9,8},{10,9},{11,10},{12... | collective-permute-start | bytes 43016 | tf_op jit(solution)/shard_map/ppermute | solution.py:20
  235.4 38.3 %collective-permute-start.56 = (bf16[1,28,256]{2,1,0:T(8,128)(2,1)}, bf16[1,28,256]{2,1,0:T(8,128)(2,1)}, u32[]{:S(2)}, u32[]{:S(2)}) collective-permute-start(bf16[1,28,256]{2,1,0:T(8,128)(2,1)} %collective-permute-done.55), channel_id=1, source_target_pairs={{0,1},{1,2},{2,3},{3,4},{4,5},{5,6},{6,7},{8,9},{9,10},{10,11},{11... | collective-permute-start | bytes 43016 | tf_op jit(solution)/shard_map/ppermute | solution.py:20
  239.1 39.6 %collective-permute-start.59 = (bf16[1,28,256]{2,1,0:T(8,128)(2,1)}, bf16[1,28,256]{2,1,0:T(8,128)(2,1)}, u32[]{:S(2)}, u32[]{:S(2)}) collective-permute-start(bf16[1,28,256]{2,1,0:T(8,128)(2,1)} %collective-permute-done.58), channel_id=1, source_target_pairs={{1,0},{2,1},{3,2},{4,3},{5,4},{6,5},{7,6},{9,8},{10,9},{11,10},{12... | collective-permute-start | bytes 43016 | tf_op jit(solution)/shard_map/ppermute | solution.py:20
  241.0 57.8 %collective-permute-start.12 = (f32[28,256]{1,0:T(8,128)}, f32[28,256]{1,0:T(8,128)}, u32[]{:S(2)}, u32[]{:S(2)}) collective-permute-start(f32[28,256]{1,0:T(8,128)} %bitcast.43), channel_id=1, source_target_pairs={{0,8},{8,16},{16,24},{24,32},{32,40},{40,48},{48,56},{56,64},{64,7... | collective-permute-start | bytes 86024 | tf_op jit(solution)/shard_map/ppermute | solution.py:20
  268.3 34.1 %collective-permute-start.14 = (f32[28,256]{1,0:T(8,128)}, f32[28,256]{1,0:T(8,128)}, u32[]{:S(2)}, u32[]{:S(2)}) collective-permute-start(f32[28,256]{1,0:T(8,128)} %bitcast.44), channel_id=1, source_target_pairs={{0,8},{8,16},{16,24},{24,32},{32,40},{40,48},{48,56},{56,64},{64,7... | collective-permute-start | bytes 86024 | tf_op jit(solution)/shard_map/ppermute | solution.py:20
  271.0 35.6 %collective-permute-start.15 = (f32[28,256]{1,0:T(8,128)}, f32[28,256]{1,0:T(8,128)}, u32[]{:S(2)}, u32[]{:S(2)}) collective-permute-start(f32[28,256]{1,0:T(8,128)} %bitcast.45), channel_id=1, source_target_pairs={{0,8},{8,16},{16,24},{24,32},{32,40},{40,48},{48,56},{56,64},{64,7... | collective-permute-start | bytes 86024 | tf_op jit(solution)/shard_map/ppermute | solution.py:20
  273.7 34.8 %collective-permute-start.17 = (f32[28,256]{1,0:T(8,128)}, f32[28,256]{1,0:T(8,128)}, u32[]{:S(2)}, u32[]{:S(2)}) collective-permute-start(f32[28,256]{1,0:T(8,128)} %bitcast.46), channel_id=1, source_target_pairs={{0,1},{1,2},{2,3},{3,4},{4,5},{5,6},{6,7},{8,9},{9,10},{10,11},{11... | collective-permute-start | bytes 86024 | tf_op jit(solution)/shard_map/ppermute | solution.py:20
  278.7 34.1 %collective-permute-start.18 = (f32[28,256]{1,0:T(8,128)}, f32[28,256]{1,0:T(8,128)}, u32[]{:S(2)}, u32[]{:S(2)}) collective-permute-start(f32[28,256]{1,0:T(8,128)} %bitcast.47), channel_id=1, source_target_pairs={{1,0},{2,1},{3,2},{4,3},{5,4},{6,5},{7,6},{9,8},{10,9},{11,10},{12... | collective-permute-start | bytes 86024 | tf_op jit(solution)/shard_map/ppermute | solution.py:20
  381.5 28.9 %collective-permute-start.36 = (f32[28,256]{1,0:T(8,128)}, f32[28,256]{1,0:T(8,128)}, u32[]{:S(2)}, u32[]{:S(2)}) collective-permute-start(f32[28,256]{1,0:T(8,128)} %bitcast.81), channel_id=1, source_target_pairs={{0,8},{8,16},{16,24},{24,32},{32,40},{40,48},{48,56},{56,64},{64,7... | collective-permute-start | bytes 86024 | tf_op jit(solution)/shard_map/ppermute | solution.py:20
  392.6 27.6 %collective-permute-start.39 = (f32[28,256]{1,0:T(8,128)}, f32[28,256]{1,0:T(8,128)}, u32[]{:S(2)}, u32[]{:S(2)}) collective-permute-start(f32[28,256]{1,0:T(8,128)} %bitcast.83), channel_id=1, source_target_pairs={{0,8},{8,16},{16,24},{24,32},{32,40},{40,48},{48,56},{56,64},{64,7... | collective-permute-start | bytes 86024 | tf_op jit(solution)/shard_map/ppermute | solution.py:20
  396.1 26.0 %collective-permute-start.41 = (f32[28,256]{1,0:T(8,128)}, f32[28,256]{1,0:T(8,128)}, u32[]{:S(2)}, u32[]{:S(2)}) collective-permute-start(f32[28,256]{1,0:T(8,128)} %bitcast.84), channel_id=1, source_target_pairs={{0,1},{1,2},{2,3},{3,4},{4,5},{5,6},{6,7},{8,9},{9,10},{10,11},{11... | collective-permute-start | bytes 86024 | tf_op jit(solution)/shard_map/ppermute | solution.py:20
  493.2 132.1 %collective-permute-start.60 = (f32[28,256]{1,0:T(8,128)}, f32[28,256]{1,0:T(8,128)}, u32[]{:S(2)}, u32[]{:S(2)}) collective-permute-start(f32[28,256]{1,0:T(8,128)} %bitcast.119), channel_id=1, source_target_pairs={{0,8},{8,16},{16,24},{24,32},{32,40},{40,48},{48,56},{56,64},{64,7... | collective-permute-start | bytes 86024 | tf_op jit(solution)/shard_map/ppermute | solution.py:20
  500.5 132.0 %collective-permute-start.62 = (f32[28,256]{1,0:T(8,128)}, f32[28,256]{1,0:T(8,128)}, u32[]{:S(2)}, u32[]{:S(2)}) collective-permute-start(f32[28,256]{1,0:T(8,128)} %bitcast.120), channel_id=1, source_target_pairs={{0,8},{8,16},{16,24},{24,32},{32,40},{40,48},{48,56},{56,64},{64,7... | collective-permute-start | bytes 86024 | tf_op jit(solution)/shard_map/ppermute | solution.py:20
  504.4 132.5 %collective-permute-start.63 = (f32[28,256]{1,0:T(8,128)}, f32[28,256]{1,0:T(8,128)}, u32[]{:S(2)}, u32[]{:S(2)}) collective-permute-start(f32[28,256]{1,0:T(8,128)} %bitcast.121), channel_id=1, source_target_pairs={{0,8},{8,16},{16,24},{24,32},{32,40},{40,48},{48,56},{56,64},{64,7... | collective-permute-start | bytes 86024 | tf_op jit(solution)/shard_map/ppermute | solution.py:20
  507.0 136.6 %collective-permute-start.65 = (f32[28,256]{1,0:T(8,128)}, f32[28,256]{1,0:T(8,128)}, u32[]{:S(2)}, u32[]{:S(2)}) collective-permute-start(f32[28,256]{1,0:T(8,128)} %bitcast.122), channel_id=1, source_target_pairs={{0,1},{1,2},{2,3},{3,4},{4,5},{5,6},{6,7},{8,9},{9,10},{10,11},{11... | collective-permute-start | bytes 86024 | tf_op jit(solution)/shard_map/ppermute | solution.py:20
  511.2 136.4 %collective-permute-start.66 = (f32[28,256]{1,0:T(8,128)S(1)}, f32[28,256]{1,0:T(8,128)}, u32[]{:S(2)}, u32[]{:S(2)}) collective-permute-start(f32[28,256]{1,0:T(8,128)S(1)} %bitcast.402), channel_id=1, source_target_pairs={{1,0},{2,1},{3,2},{4,3},{5,4},{6,5},{7,6},{9,8},{10,9},{11,10},{12... | collective-permute-start | bytes 86024 | tf_op jit(solution)/shard_map/ppermute | solution.py:20
  625.3 26.0 %collective-permute-start.67 = (f32[28,256]{1,0:T(8,128)}, f32[28,256]{1,0:T(8,128)}, u32[]{:S(2)}, u32[]{:S(2)}) collective-permute-start(f32[28,256]{1,0:T(8,128)} %bitcast.124), channel_id=1, source_target_pairs={{8,0},{16,8},{24,16},{32,24},{40,32},{48,40},{56,48},{64,56},{72,6... | collective-permute-start | bytes 86024 | tf_op jit(solution)/shard_map/ppermute | solution.py:20
  636.9 26.6 %collective-permute-start.69 = (f32[28,256]{1,0:T(8,128)}, f32[28,256]{1,0:T(8,128)S(1)}, u32[]{:S(2)}, u32[]{:S(2)}) collective-permute-start(f32[28,256]{1,0:T(8,128)} %bitcast.125), channel_id=1, source_target_pairs={{8,0},{16,8},{24,16},{32,24},{40,32},{48,40},{56,48},{64,56},{72,6... | collective-permute-start | bytes 86024 | tf_op jit(solution)/shard_map/ppermute | solution.py:20
  (193 other events, 2855.4 us)
